TPU v7x, 128 devices: a whole 4x4x4 slice. The times are simulated.
128 devices in a mesh: db: 8 (over z, x_lo), tp: 16 (over y, x_hi, core).
Axes of the slice: x: 4 (x_hi: 2, x_lo: 2; x = x_hi * 2 + x_lo), y: 4, z: 4, core: 2. Of those that a mesh axis runs over, the one named last changes fastest.
Arguments:
- queries: bfloat16 [32768, 1024], P('db', 'tp'), may hold values from -6 to 6
- enc_up: bfloat16 [1024, 4096], P(None, 'tp'), may hold values from -0.1875 to 0.1875
- enc_down: bfloat16 [4096, 1024], P('tp'), may hold values from -0.09375 to 0.09375
- attn_gain: float32 [1024], replicated, may hold values from 0.25 to 1.75
- w_query: bfloat16 [1024, 1024], P(None, 'tp'), may hold values from -0.1875 to 0.1875
- w_keyval: bfloat16 [2, 1024, 1024], replicated, may hold values from -0.1875 to 0.1875
- w_out: bfloat16 [1024, 1024], P('tp'), may hold values from -0.1875 to 0.1875
- database: float32 [2048, 128, 1024], P('db', 'tp'), may hold values from -6 to 6
- nb_owner: int32 [512, 2], P('db'), may hold values from 0 to 7, as said below
- nb_row: int32 [512, 2], P('db'), may hold values from 0 to 255
Outputs:
- mixed: bfloat16 [32768, 1024], P('db', 'tp')
Inputs may be any that keep to these rules, and one draw needn't show every extreme that they name: `nb_owner`: among the neighbour ids of one db index's 64 stretches, no owner is named more than 32 times, and some owner is named exactly 32 times.
All inputs are finite; a program needn't handle non-finite values.
Results may differ from a plain program's by a relative error of at most 0.02.
Values may be sent and summed in bfloat16 or wider, within the bound.
A program may use at most 128 MiB of HBM per device.

v0:
```python
import jax
import jax.numpy as jnp
from jax import lax
from jax.sharding import PartitionSpec as P

HEAD_DIM = 64
STRETCH = 64


def per_device(
    queries, enc_up, enc_down, attn_gain, w_query, w_keyval, w_out, database, nb_owner, nb_row
):
    db_count = lax.axis_size("db")
    width = queries.shape[1]
    full_q = lax.all_gather(queries, "tp", axis=1, tiled=True)
    hidden = jax.nn.gelu(
        jnp.dot(full_q, enc_up, preferred_element_type=jnp.float32), approximate=True
    ).astype(jnp.bfloat16)
    partial_value = jnp.dot(hidden, enc_down, preferred_element_type=jnp.float32)
    summed = lax.psum(partial_value.astype(jnp.bfloat16), "tp").astype(jnp.float32)
    encoded = (full_q.astype(jnp.float32) + summed).astype(jnp.bfloat16)
    enc_slice = lax.dynamic_slice_in_dim(encoded, lax.axis_index("tp") * width, width, 1)
    enc_float = encoded.astype(jnp.float32)
    scale_row = lax.rsqrt(jnp.mean(enc_float * enc_float, axis=1, keepdims=True) + 1e-06)
    normed = (enc_float * scale_row * attn_gain[None, :]).astype(jnp.bfloat16)
    query_heads = jnp.dot(normed, w_query, preferred_element_type=jnp.float32).astype(jnp.bfloat16)
    stretches = nb_owner.shape[0]
    per_group = stretches * nb_owner.shape[1]
    capacity = per_group // 4
    owners = nb_owner.reshape(-1)
    rows = nb_row.reshape(-1)
    one_hot = (owners[:, None] == jnp.arange(db_count, dtype=jnp.int32)[None, :]).astype(jnp.int32)
    rank = jnp.sum((jnp.cumsum(one_hot, axis=0) - one_hot) * one_hot, axis=1)
    send_rows = jnp.zeros((db_count, capacity), jnp.int32).at[owners, rank].set(rows)
    found = database[
        lax.all_to_all(send_rows, "db", split_axis=0, concat_axis=0, tiled=True)
    ].astype(jnp.bfloat16)
    replies = lax.all_to_all(found, "db", split_axis=0, concat_axis=0, tiled=True)
    neighbours = replies[owners, rank]
    keyval = jnp.einsum(
        "mtd,sde->smte", neighbours, w_keyval, preferred_element_type=jnp.float32
    ).astype(jnp.bfloat16)
    keyval = lax.all_to_all(keyval, "tp", split_axis=3, concat_axis=2, tiled=True)
    local_heads = keyval.shape[3] // HEAD_DIM
    span = keyval.shape[1] // stretches * keyval.shape[2]
    keys = keyval[0].reshape(stretches, span, local_heads, HEAD_DIM)
    values = keyval[1].reshape(stretches, span, local_heads, HEAD_DIM)
    heads_q = query_heads.reshape(stretches, STRETCH, local_heads, HEAD_DIM)
    scores = jnp.einsum(
        "cqhd,ckhd->chqk", heads_q, keys, preferred_element_type=jnp.float32
    ) * HEAD_DIM ** (-0.5)
    weights = jax.nn.softmax(scores, axis=-1).astype(jnp.bfloat16)
    context = jnp.einsum(
        "chqk,ckhd->cqhd", weights, values, preferred_element_type=jnp.float32
    ).astype(jnp.bfloat16)
    context = context.reshape(stretches * STRETCH, local_heads * HEAD_DIM)
    projected = jnp.dot(context, w_out, preferred_element_type=jnp.float32)
    out_share = lax.psum_scatter(
        projected.astype(jnp.bfloat16), "tp", scatter_dimension=1, tiled=True
    ).astype(jnp.float32)
    return (enc_slice.astype(jnp.float32) + out_share).astype(jnp.bfloat16)


def solution(mesh):
    placed = (
        P("db", "tp"),
        P(None, "tp"),
        P("tp", None),
        P(),
        P(None, "tp"),
        P(),
        P("tp", None),
        P("db", "tp", None),
        P("db", None),
        P("db", None),
    )
    return jax.shard_map(
        per_device, mesh=mesh, in_specs=placed, out_specs=P("db", "tp"), check_vma=False
    )
```

profile of v0, /device:TPU:1, one launch (start us, length us, event | category | flops | bytes accessed | tf_op | source)
XLA Modules:
  0.0 511.5 jit_solution(9371730551459799229)
XLA Ops:
  6.5 0.0 copy-start
  6.5 0.0 all-gather.2.cloned.1.call-start
  6.5 0.7 all-gather.2.cloned.1.call-update
  7.3 0.8 copy.49
  8.0 0.1 eq.15
  8.2 0.1 reshape.127
  8.3 0.8 copy.51
  9.1 0.1 reshape.149
  9.2 0.1 fusion.36
  9.3 0.2 reduce_window_sum.11
  9.5 0.2 select_reduce_fusion
  9.7 6.4 %scatter_fusion = s32[8,32]{1,0:T(8,128)S(1)} fusion(s32[8,32]{1,0:T(8,128)S(1)} %broadcast.78, s32[128]{0:T(128)S(1)} %get-tuple-element.7, s32[128]{0:T(128)S(1)} %reshape.149), kind=kCustom, calls=%fused_computation.2 | custom fusion | bytes 2560 | tf_op jit(solution)/shard_map/scatter | solution.py:34
  16.1 11.6 %all_to_all.32 = s32[8,1,32]{2,1,0:T(1,128)S(1)} all-to-all(s32[8,1,32]{2,1,0:T(1,128)S(1)} %bitcast.52), channel_id=1, replica_groups=mesh['db'=8,'tp'=16] {'db'}, dimensions={0} | all-to-all | bytes 2048 | tf_op jit(solution)/shard_map/all_to_all | solution.py:36
  27.7 0.1 reshape.135
  27.7 6.3 %gather_fusion = bf16[256,8,1024]{2,1,0:T(8,128)(2,1)} fusion(f32[256,8,1024]{2,1,0:T(8,128)} %param.17, s32[1024]{0:T(1024)S(1)} %pad_clamp_fusion), kind=kCustom, calls=%fused_computation | custom fusion | bytes 8389632 | tf_op jit(solution)/shard_map/gather | solution.py:35
  34.1 0.0 copy-start.5
  34.1 4.7 all-to-all-start.1
  38.8 0.0 all-reduce.2.cloned.1.call-start
  38.9 70.3 %all-gather.2.cloned.1.call-done = bf16[4096,1024]{0,1:T(8,128)(2,1)} async-done(((bf16[4096,64]{0,1:T(8,128)(2,1)}), bf16[4096,1024]{0,1:T(8,128)(2,1)}) %all-gather.2.cloned.1.call-update) | async-done | bytes 8388624 | tf_op jit(solution)/shard_map/all_gather | solution.py:15
  109.2 0.0 copy-done
  109.2 0.0 copy-done.5
  109.2 12.6 %convolution_convert_fusion = bf16[4096,1024]{0,1:T(8,128)(2,1)} fusion(bf16[256,1024]{1,0:T(8,128)(2,1)S(1)} %copy-done, bf16[4096,1024]{0,1:T(8,128)(2,1)} %all-gather.2.cloned.1.call-done, bf16[1024,256]{1,0:T(8,128)(2,1)S(1)} %copy-done.5), kind=kOutput, calls=%fused_computation.14 | convolution fusion | flops 4308598784 | bytes 17825792 | tf_op jit(solution)/shard_map/dot_general | solution.py:19
  121.8 0.0 all-reduce.2.cloned.1.call-update
  121.8 0.0 reduce-scatter.4.cloned.1.call-start
  121.9 0.0 all-to-all-done.1
  121.9 3.0 gather_fusion.1
  125.0 8.5 %convert_bitcast_fusion.1 = bf16[2,128,8,1024]{3,1,0,2:T(8,128)(2,1)} fusion(bf16[2,1024,1024]{2,1,0:T(8,128)(2,1)} %param.15, bf16[128,8,1024,1]{2,1,0,3:T(8,128)(2,1)S(1)} %bitcast.59), kind=kOutput, calls=%fused_computation.29 | convolution fusion | flops 4297064448 | bytes 10485760 | tf_op jit(solution)/shard_map/mtd,sde->smte/dot_general | solution.py:40
  133.5 11.3 %copy.54 = bf16[2,128,8,1024]{1,0,2,3:T(2,128)(2,1)} copy(bf16[2,128,8,1024]{3,1,0,2:T(8,128)(2,1)} %convert_bitcast_fusion.1) | data formatting | bytes 8388608 | tf_op jit(solution)/shard_map/convert_element_type | solution.py:42
  144.7 100.4 %all_to_all.33 = bf16[2,128,8,1024]{1,0,2,3:T(2,128)(2,1)S(1)} all-to-all(bf16[2,128,8,1024]{1,0,2,3:T(2,128)(2,1)} %copy.54), channel_id=1, replica_groups=mesh['db'=8,'tp'=16] {'tp'}, dimensions={3} | all-to-all | bytes 8388608 | tf_op jit(solution)/shard_map/all_to_all | solution.py:43
  245.1 1.1 copy.55
  246.2 2.4 fusion.52
  248.5 7.5 %copy.57 = bf16[1,128,16,8,64]{4,3,2,1,0:T(8,128)(2,1)} copy(bf16[1,128,16,8,64]{1,4,2,3,0:T(8,128)(2,1)} %get-tuple-element.9) | data formatting | bytes 4194304 | tf_op jit(solution)/shard_map/slice | solution.py:46
  256.0 6.5 %copy.56 = bf16[1,128,16,8,64]{4,3,2,1,0:T(8,128)(2,1)} copy(bf16[1,128,16,8,64]{1,4,2,3,0:T(8,128)(2,1)S(1)} %get-tuple-element.10) | data formatting | bytes 4194304 | tf_op jit(solution)/shard_map/slice | solution.py:47
  262.5 0.0 copy-start.6
  262.5 0.0 copy-start.7
  262.5 97.2 %all-reduce.2.cloned.1.call-done = bf16[4096,1024]{0,1:T(8,128)(2,1)} async-done(((bf16[4096,1024]{0,1:T(8,128)(2,1)}), bf16[4096,1024]{0,1:T(8,128)(2,1)}) %all-reduce.2.cloned.1.call-update) | async-done | bytes 8388624 | tf_op jit(solution)/shard_map/psum | solution.py:20
  359.6 8.3 %fusion.1 = (f32[4096]{0:T(1024)S(1)}, bf16[4096,1024]{0,1:T(8,128)(2,1)S(1)}) fusion(bf16[4096,1024]{0,1:T(8,128)(2,1)} %all-reduce.2.cloned.1.call-done, bf16[4096,1024]{0,1:T(8,128)(2,1)} %all-gather.2.cloned.1.call-done), kind=kLoop, calls=%fused_computation.6 | loop fusion | flops 29356032 | bytes 25182208 | tf_op jit(solution)/shard_map/reduce_sum | solution.py:24
  367.9 0.0 copy-start.2
  368.0 3.2 copy-done.2
  371.2 0.0 copy-done.6
  371.2 0.0 copy-done.7
  371.2 2.5 fusion.8
  373.6 0.5 copy.70
  374.1 3.7 fusion.56
  377.9 0.0 copy-start.3
  377.9 2.0 copy-done.3
  379.9 1.4 fusion.53
  381.3 0.0 copy-start.4
  381.3 13.5 %fusion.35 = bf16[64,64,1,64]{1,3,0,2:T(8,128)(2,1)S(1)} fusion(bf16[64,256,64]{2,1,0:T(8,128)(2,1)} %bitcast.58, f32[64,64]{1,0:T(8,128)S(1)} %fusion.53, f32[64,64,256]{2,1,0:T(8,128)} %copy-done.3), kind=kOutput, calls=%fused_computation.40 | convolution fusion | flops 139727104 | bytes 6832128 | tf_op jit(solution)/shard_map/chqk,ckhd->cqhd/dot_general | solution.py:53
  394.8 0.7 copy.61
  395.5 0.8 reshape.132
  396.3 0.0 copy-done.4
  396.3 5.6 %convert_bitcast_fusion = bf16[1024,4096]{1,0:T(8,128)(2,1)} fusion(bf16[4096,64]{0,1:T(8,128)(2,1)S(1)} %reshape.132, bf16[64,1024]{1,0:T(8,128)(2,1)S(1)} %copy-done.4), kind=kOutput, calls=%fused_computation.11 | convolution fusion | flops 541065216 | bytes 9043968 | tf_op jit(solution)/shard_map/dot_general | solution.py:57
  401.9 0.0 copy-start.1
  401.9 0.0 reduce-scatter.4.cloned.1.call-update
  401.9 100.9 %reduce-scatter.4.cloned.1.call-done = bf16[64,4096]{1,0:T(8,128)(2,1)} async-done(((bf16[1024,4096]{1,0:T(8,128)(2,1)}), bf16[64,4096]{1,0:T(8,128)(2,1)}) %reduce-scatter.4.cloned.1.call-update) | async-done | bytes 524304
  502.8 2.1 add_convert_fusion.1
  504.9 0.0 copy-done.1
  (5 shorter events, 0.0 us)
Async XLA Ops:
  6.5 102.7 %copy-start = (bf16[256,1024]{1,0:T(8,128)(2,1)S(1)}, bf16[256,1024]{1,0:T(8,128)(2,1)}, u32[]{:S(2)}) copy-start(bf16[256,1024]{1,0:T(8,128)(2,1)} %param.12) | copy-start | bytes 1572868
  6.5 102.7 %all-gather.2.cloned.1.call-start = ((), (), s32[]{:S(2)}) async-start(), calls=%async_computation.4 | async-start | bytes 8912896 | tf_op jit(solution)/shard_map/all_gather | solution.py:15
  34.1 75.1 %copy-start.5 = (bf16[1024,256]{1,0:T(8,128)(2,1)S(1)}, bf16[1024,256]{1,0:T(8,128)(2,1)}, u32[]{:S(2)}) copy-start(bf16[1024,256]{1,0:T(8,128)(2,1)} %param.11) | copy-start | bytes 1572868
  34.1 87.8 %all-to-all-start.1 = ((bf16[8,32,8,1024]{3,2,1,0:T(8,128)(2,1)}), bf16[8,32,8,1024]{3,2,1,0:T(8,128)(2,1)}, u32[]{:S(2)}, u32[]{:S(2)}) async-start(bf16[8,32,8,1024]{3,2,1,0:T(8,128)(2,1)} %bitcast.55), calls=%async_computation.1 | async-start | bytes 8388608 | tf_op jit(solution)/shard_map/all_to_all | solution.py:38
  38.8 320.8 %all-reduce.2.cloned.1.call-start = ((), (), s32[]{:S(2)}) async-start(), calls=%async_computation.5 | async-start | bytes 16777216 | tf_op jit(solution)/shard_map/psum | solution.py:20
  121.8 381.0 %reduce-scatter.4.cloned.1.call-start = ((), (), s32[]{:S(2)}) async-start(), calls=%async_computation.6 | async-start | bytes 8912896
  262.5 108.7 %copy-start.6 = (bf16[1024,64]{0,1:T(8,128)(2,1)S(1)}, bf16[1024,64]{0,1:T(8,128)(2,1)}, u32[]{:S(2)}) copy-start(bf16[1024,64]{0,1:T(8,128)(2,1)} %param.14) | copy-start | bytes 393220
  262.5 108.7 %copy-start.7 = (f32[1024]{0:T(1024)S(1)}, f32[1024]{0:T(1024)}, u32[]{:S(2)}) copy-start(f32[1024]{0:T(1024)} %param.13) | copy-start | bytes 12292
  367.9 3.2 copy-start.2
  377.9 2.0 copy-start.3
  381.3 15.0 %copy-start.4 = (bf16[64,1024]{1,0:T(8,128)(2,1)S(1)}, bf16[64,1024]{1,0:T(8,128)(2,1)}, u32[]{:S(2)}) copy-start(bf16[64,1024]{1,0:T(8,128)(2,1)} %param.16) | copy-start | bytes 393220
  401.9 103.0 %copy-start.1 = (bf16[256,1024]{1,0:T(8,128)(2,1)S(1)}, bf16[256,1024]{1,0:T(8,128)(2,1)}, u32[]{:S(2)}) copy-start(bf16[256,1024]{1,0:T(8,128)(2,1)} %param.12) | copy-start | bytes 1572868
Sparse Core Ops, SparseCore 0:
  9.8 99.3 all-gather.1
  122.0 237.6 all-reduce.1
  402.1 100.7 reduce-scatter.3
where the time goes:
time: 513 us; the launch traced here: 511 us
  waiting for transfers between devices  269 us (52%)
  blocking collectives  112 us (22%)
  local copies, waits for them, and re-layouts  53.6 us (10%)
  matrix products  46.4 us (9%)
  between operations  13.3 us (3%)
  other arithmetic  12.3 us (2%)
    unnamed x4, waiting for transfers between devices  102 us
    all_to_all x1, blocking collectives, per_device(): lax.all_to_all(keyval, 'tp', split_axis=3, concat_axis=2, tiled=True)  100 us
    psum x1, waiting for transfers between devices, per_device(): lax.psum(partial_value.astype(jnp.bfloat16), 'tp').astype(jnp.float32)  97.2 us
    all_gather x1, waiting for transfers between devices, per_device(): full_q = lax.all_gather(queries, 'tp', axis=1, tiled=True)  70.3 us
    dot_general x1, matrix products, per_device(): jnp.einsum('chqk,ckhd->cqhd', weights, values, preferred_element_type=jnp...  13.5 us
    dot_general x1, matrix products, per_device(): jnp.dot(hidden, enc_down, preferred_element_type=jnp.float32)  12.6 us
    all_to_all x1, blocking collectives, per_device(): lax.all_to_all(send_rows, 'db', split_axis=0, concat_axis=0, tiled=True)  11.6 us
    convert_element_type x1, local copies, waits for them, and re-layouts, per_device(): keyval = jnp.einsum('mtd,sde->smte', neighbours, w_keyval, preferred_elem...  11.3 us
  transfers between devices with their start and end apart: 4, of which 3 were waited for; matrix products, arithmetic and copies ran while one was open for 13% of the time, Pallas kernels for 0%

commit v1 on v0

v1 whole, which is shorter than its diff:
```python
import jax
import jax.numpy as jnp
from jax import lax
from jax.experimental import pallas as pl
from jax.experimental.pallas import tpu as pltpu
from jax.sharding import PartitionSpec as P

MESH = pl.DeviceIdType.MESH
BF = jnp.bfloat16
F32 = jnp.float32
ANY = pl.BlockSpec(memory_space=pl.ANY)
VM = pl.BlockSpec(memory_space=pltpu.VMEM)
SM = pl.BlockSpec(memory_space=pltpu.SMEM)


def place():
    d = lax.axis_index("db")
    t = lax.axis_index("tp")
    return d, t, d % 2, t // 4, (t // 2) % 2, t % 2


def greet(peers):
    sem = pltpu.get_barrier_semaphore()
    for peer in peers:
        pl.semaphore_signal(sem, inc=1, device_id=peer, device_id_type=MESH)
    pl.semaphore_wait(sem, len(peers))


def remote(src, dst, send, recv, dev):
    return pltpu.make_async_remote_copy(
        src_ref=src, dst_ref=dst, send_sem=send, recv_sem=recv, device_id=dev, device_id_type=MESH
    )


def in_kernel(
    slot, want, qt, up, down, wqt, wo, base,
    xbuf, upall, downall, wqall, woall, near,
    basev, sbuf, rbuf, pbuf, asked, asked_s,
    base_sem, ask_s, ask_r, ask_l, q_s, q_r, q_l, w_s, w_r, w_l, f_s, f_r, h_s, h_r, hf_s, hf_r,
    a_s, a_r, b_s, b_r, b_l,
):
    d, t, xlo, y, xhi, c = place()
    sib = t + 1 - 2 * c
    load = pltpu.make_async_copy(base, basev, base_sem)
    load.start()
    db_peers = [lax.rem(d + k, 8) for k in (4, 5, 3, 2, 6, 7, 1)]
    tp_peers = [lax.rem(t + k, 16) for k in range(1, 16)]
    y_peers = [lax.rem(t + 4 * k, 16) for k in (1, 3, 2)]
    across = (d + 1 - 2 * xlo, t + 2 - 4 * xhi)
    greet([(g, t) for g in db_peers] + [(d, s) for s in tp_peers] + [across])

    waits = []
    asks = []
    for i, g in enumerate(db_peers):
        cp = remote(want.at[g], asked.at[d], ask_s.at[i], ask_r.at[d], (g, t))
        cp.start()
        asks.append((cp, g))
    own_ask = pltpu.make_async_copy(want.at[d], asked.at[d], ask_l.at[0])
    own_ask.start()

    mine = 2 * y + c
    for i, s in enumerate(y_peers):
        for j, (src, dst, at) in enumerate(
            ((up, upall, mine), (down, downall, mine), (wqt, wqall, t), (wo, woall, t))
        ):
            cp = remote(src, dst.at[at], w_s.at[4 * i + j], w_r.at[4 * y + j], (d, s))
            cp.start()
            waits.append(cp.wait_send)
    own = []
    for j, (src, dst, at) in enumerate(
        ((up, upall, mine), (down, downall, mine), (wqt, wqall, t), (wo, woall, t))
    ):
        cp = pltpu.make_async_copy(src, dst.at[at], w_l.at[j])
        cp.start()
        own.append(cp)
        cp = remote(src, dst.at[at], f_s.at[4 * y + j], f_r.at[4 * y + j], (d, sib))
        cp.start()
        waits.append(cp.wait_send)

    for i, s in enumerate(tp_peers):
        to = (s // 4) * 4 + s % 2
        for p in range(2):
            col = pl.multiple_of(256 * (to + 2 * p), 256)
            cp = remote(
                qt.at[:, pl.ds(col, 256)],
                xbuf.at[p, pl.ds(pl.multiple_of(64 * t, 64), 64), :],
                q_s.at[2 * i + p], q_r.at[2 * t + p], (d, s),
            )
            cp.start()
            waits.append(cp.wait_send)
    for p in range(2):
        col = pl.multiple_of(256 * (4 * y + c + 2 * p), 256)
        cp = pltpu.make_async_copy(
            qt.at[:, pl.ds(col, 256)],
            xbuf.at[p, pl.ds(pl.multiple_of(64 * t, 64), 64), :], q_l.at[p])
        cp.start()
        own.append(cp)

    own_ask.wait()
    for cp, g in asks:
        cp.wait_send()
        remote(want.at[d], asked.at[g], ask_s.at[0], ask_r.at[g], (g, t)).wait_recv()
    to_s = pltpu.make_async_copy(asked, asked_s, ask_l.at[1])
    to_s.start()
    to_s.wait()
    load.wait()

    def pack(g, dst, at):
        def body(r, carry):
            dst[at, r] = basev[asked_s[g, 0, r]].astype(BF)
            return carry
        lax.fori_loop(0, 32, body, 0, unroll=4)

    for i, g in enumerate(db_peers):
        pack(g, sbuf, g)
        cp = remote(sbuf.at[g], rbuf.at[d], a_s.at[i], a_r.at[d], (g, t))
        cp.start()
        waits.append(cp.wait_send)
    pack(d, rbuf, d)

    for cp in own:
        cp.wait()
    across_waits = []
    for j, (src, dst) in enumerate(((wqt, wqall), (wo, woall))):
        cp = remote(src, dst.at[t], h_s.at[2 * y + j], h_r.at[2 * y + j], across)
        cp.start()
        waits.append(cp.wait_send)
    for i, s in enumerate(y_peers):
        ys = s // 4
        for j, (src, dst, at) in enumerate(
            ((up, upall, 2 * ys + c), (down, downall, 2 * ys + c), (wqt, wqall, s), (wo, woall, s))
        ):
            remote(src, dst.at[at], w_s.at[0], w_r.at[4 * ys + j], (d, s)).wait_recv()
            cp = remote(dst.at[at], dst.at[at], f_s.at[4 * ys + j], f_r.at[4 * ys + j], (d, sib))
            cp.start()
            waits.append(cp.wait_send)
            if j >= 2:
                cp = remote(dst.at[at], dst.at[at], h_s.at[2 * ys + j - 2], h_r.at[2 * ys + j - 2], across)
                cp.start()
                waits.append(cp.wait_send)
    for ys in range(4):
        for j, (src, dst) in enumerate(((wqt, wqall), (wo, woall))):
            at = 4 * ys + 2 * (1 - xhi) + c
            remote(src, dst.at[at], h_s.at[0], h_r.at[2 * ys + j], across).wait_recv()
            cp = remote(dst.at[at], dst.at[at], hf_s.at[2 * ys + j], hf_r.at[2 * ys + j], (d, sib))
            cp.start()
            waits.append(cp.wait_send)

    for i, g in enumerate(db_peers):
        remote(sbuf.at[g], rbuf.at[g], a_s.at[0], a_r.at[g], (g, t)).wait_recv()
    for i, s in enumerate(tp_peers):
        for b in range(8):
            k = slot[s * 8 + b]
            pbuf[s, b] = rbuf[k // 32, k % 32]
        cp = remote(pbuf.at[s], near.at[:, t], b_s.at[i], b_r.at[t], (d, s))
        cp.start()
        waits.append(cp.wait_send)
    for b in range(8):
        k = slot[t * 8 + b]
        pbuf[t, b] = rbuf[k // 32, k % 32]
    last = pltpu.make_async_copy(pbuf.at[t], near.at[:, t], b_l.at[0])
    last.start()

    for s in tp_peers:
        for p in range(2):
            remote(
                qt.at[:, pl.ds(0, 256)], xbuf.at[p, pl.ds(pl.multiple_of(64 * s, 64), 64), :],
                q_s.at[0], q_r.at[2 * s + p], (d, s)).wait_recv()
        remote(pbuf.at[s], near.at[:, s], b_s.at[0], b_r.at[s], (d, s)).wait_recv()
    for ys in range(4):
        for j, (src, dst, at) in enumerate(
            ((up, upall, 2 * ys + 1 - c), (down, downall, 2 * ys + 1 - c),
             (wqt, wqall, 4 * ys + 2 * xhi + 1 - c), (wo, woall, 4 * ys + 2 * xhi + 1 - c))
        ):
            remote(src, dst.at[at], f_s.at[0], f_r.at[4 * ys + j], (d, sib)).wait_recv()
        for j, (src, dst) in enumerate(((wqt, wqall), (wo, woall))):
            at = 4 * ys + 2 * (1 - xhi) + 1 - c
            remote(src, dst.at[at], hf_s.at[0], hf_r.at[2 * ys + j], (d, sib)).wait_recv()
    last.wait()
    for w in waits:
        w()


def fetch(slot, want, qt, up, down, wqt, wo, base):
    D = pltpu.SemaphoreType.DMA
    return pl.pallas_call(
        in_kernel,
        name="fetch",
        out_shape=(
            jax.ShapeDtypeStruct((2, 1024, 256), BF),
            jax.ShapeDtypeStruct((8, 1024, 256), BF),
            jax.ShapeDtypeStruct((8, 256, 1024), BF),
            jax.ShapeDtypeStruct((16, 64, 1024), BF),
            jax.ShapeDtypeStruct((16, 64, 1024), BF),
            jax.ShapeDtypeStruct((8, 16, 8, 1024), BF),
        ),
        in_specs=[SM, VM, ANY, ANY, ANY, ANY, ANY, ANY],
        out_specs=(ANY,) * 6,
        scratch_shapes=[
            pltpu.VMEM((256, 8, 1024), F32),
            pltpu.VMEM((8, 32, 8, 1024), BF),
            pltpu.VMEM((8, 32, 8, 1024), BF),
            pltpu.VMEM((16, 8, 8, 1024), BF),
            pltpu.VMEM((8, 8, 128), jnp.int32),
            pltpu.SMEM((8, 8, 128), jnp.int32),
            D, D((7,)), D((8,)), D((2,)), D((30,)), D((32,)), D((2,)),
            D((12,)), D((16,)), D((4,)), D((16,)), D((16,)),
            D((8,)), D((8,)), D((8,)), D((8,)),
            D((7,)), D((8,)), D((15,)), D((16,)), D((1,)),
        ],
        compiler_params=pltpu.CompilerParams(
            collective_id=0, has_side_effects=True, vmem_limit_bytes=56 << 20
        ),
    )(slot, want, qt, up, down, wqt, wo, base)


def swap_kernel(part, out, s, r):
    d, t, xlo, y, xhi, c = place()
    other = (d, t + 2 - 4 * xhi)
    greet([other])
    cp = remote(part.at[1 - xhi], out, s, r, other)
    cp.start()
    cp.wait()


def swap(part):
    return pl.pallas_call(
        swap_kernel,
        name="swap",
        out_shape=jax.ShapeDtypeStruct((256, 1024), BF),
        in_specs=[ANY],
        out_specs=ANY,
        scratch_shapes=[pltpu.SemaphoreType.DMA, pltpu.SemaphoreType.DMA],
        compiler_params=pltpu.CompilerParams(collective_id=1, has_side_effects=True),
    )(part)


def out_kernel(mixed, out, send, recv, own):
    d, t, xlo, y, xhi, c = place()
    peers = [lax.rem(t + k, 16) for k in range(1, 16)]
    greet([(d, s) for s in peers])
    col = pl.ds(pl.multiple_of(256 * t, 256), 256)
    cps = []
    for i, s in enumerate(peers):
        cp = remote(mixed.at[s], out.at[:, col], send.at[i], recv.at[t], (d, s))
        cp.start()
        cps.append(cp)
    lc = pltpu.make_async_copy(mixed.at[t], out.at[:, col], own)
    lc.start()
    for i, s in enumerate(peers):
        cps[i].wait_send()
        remote(
            mixed.at[s], out.at[:, pl.ds(pl.multiple_of(256 * s, 256), 256)],
            send.at[0], recv.at[s], (d, s)).wait_recv()
    lc.wait()


def give(mixed):
    D = pltpu.SemaphoreType.DMA
    return pl.pallas_call(
        out_kernel,
        name="give",
        out_shape=jax.ShapeDtypeStruct((64, 4096), BF),
        in_specs=[ANY],
        out_specs=ANY,
        scratch_shapes=[D((15,)), D((16,)), D],
        compiler_params=pltpu.CompilerParams(collective_id=2, has_side_effects=True),
    )(mixed)


def per_device(
    queries, enc_up, enc_down, attn_gain, w_query, w_keyval, w_out, database, nb_owner, nb_row
):
    owners = nb_owner.reshape(128)
    rows = nb_row.reshape(128)
    i = jnp.arange(128)
    rank = jnp.sum(
        ((owners[:, None] == owners[None, :]) & (i[None, :] < i[:, None])).astype(jnp.int32), axis=1)
    slot = owners * 32 + rank
    lane = jnp.arange(128)
    key = jnp.where(lane < 32, lane, -1)[None, :] + 32 * jnp.arange(8)[:, None]
    key = jnp.where((lane < 32)[None, :], key, -1)
    want = jnp.sum(
        jnp.where(key[:, :, None] == slot[None, None, :], rows[None, None, :], 0), axis=2)
    want = jnp.broadcast_to(want[:, None, :], (8, 8, 128))
    x, up, down, wq, wo, near = fetch(
        slot, want, queries.T, enc_up, enc_down, w_query.T, w_out, database)
    xhi = (lax.axis_index("tp") // 2) % 2
    hidden = jax.nn.gelu(
        jnp.einsum("pft,kfh->ptkh", x, up, preferred_element_type=F32), approximate=True).astype(BF)
    part = jnp.einsum("ptkh,khd->ptd", hidden, down, preferred_element_type=F32)
    other = swap(part.astype(BF))
    part_own = lax.dynamic_index_in_dim(part, xhi, 0, keepdims=False)
    x_own = lax.dynamic_index_in_dim(x, xhi, 0, keepdims=False).T
    encoded = (x_own.astype(F32) + (part_own + other.astype(F32))).astype(BF)
    ef = encoded.astype(F32)
    scale = lax.rsqrt(jnp.mean(ef * ef, axis=1, keepdims=True) + 1e-06)
    normed = (ef * scale * attn_gain[None, :]).astype(BF)
    q = jnp.einsum("td,ed->te", normed, wq.reshape(1024, 1024), preferred_element_type=F32).astype(BF)
    kv = jnp.einsum("td,sde->ste", near.reshape(1024, 1024), w_keyval, preferred_element_type=F32).astype(BF)
    k = kv[0].reshape(4, 256, 16, 64)
    v = kv[1].reshape(4, 256, 16, 64)
    qh = q.reshape(4, 64, 16, 64)
    scores = jnp.einsum("cqhd,ckhd->chqk", qh, k, preferred_element_type=F32) * 0.125
    w = jax.nn.softmax(scores, axis=-1).astype(BF)
    ctx = jnp.einsum("chqk,ckhd->cqhd", w, v, preferred_element_type=F32).astype(BF).reshape(256, 1024)
    out = jnp.dot(ctx, wo.reshape(1024, 1024), preferred_element_type=F32)
    mixed = (ef + out).astype(BF)
    return give(mixed.T.reshape(16, 64, 256)).T


def solution(mesh):
    placed = (
        P("db", "tp"),
        P(None, "tp"),
        P("tp", None),
        P(),
        P(None, "tp"),
        P(),
        P("tp", None),
        P("db", "tp", None),
        P("db", None),
        P("db", None),
    )
    return jax.shard_map(
        per_device, mesh=mesh, in_specs=placed, out_specs=P("db", "tp"), check_vma=False
    )
```

time: 513 us -> 219 us (0.43)
  waiting for transfers between devices: 269 us -> 0 us
  Pallas kernels: 0 us -> 152 us
  blocking collectives: 112 us -> 0 us
  local copies, waits for them, and re-layouts: 53.6 us -> 23.2 us
  between operations: 13.3 us -> 0.19 us
  other arithmetic: 12.3 us -> 3.77 us
  matrix products: 46.4 us -> 39.7 us
    pallas_call x0 -> x3, Pallas kernels: none -> 152 us  [the longest x1 117 us: fetch(): pl.pallas_call(in_kernel, name='fetch', out_shape=(jax.ShapeDtypeStruct((...]
    all_to_all x2 -> x0, blocking collectives: 112 us -> none  [the longest x1 100 us: per_device(): lax.all_to_all(keyval, 'tp', split_axis=3, concat_axis=2, tiled=True)]
    unnamed x4 -> x0, waiting for transfers between devices: 102 us -> none
    psum x1 -> x0, waiting for transfers between devices: 97.2 us -> none  [per_device(): lax.psum(partial_value.astype(jnp.bfloat16), 'tp').astype(jnp.float32)]
    all_gather x1 -> x0, waiting for transfers between devices: 70.3 us -> none  [per_device(): full_q = lax.all_gather(queries, 'tp', axis=1, tiled=True)]
    slice x3 -> x1, local copies, waits for them, and re-layouts: 16.3 us -> 1.77 us  [per_device(): v = kv[1].reshape(4, 256, 16, 64)]
    convert_element_type x2 -> x1, local copies, waits for them, and re-layouts: 12 us -> 0.98 us  [per_device(): jnp.einsum('chqk,ckhd->cqhd', w, v, preferred_element_type=F32).astype(BF)]
    another operation x2, local copies, waits for them, and re-layouts: 0.48 us -> 10.3 us  [the longest x1 6.37 us: per_device(): v = kv[1].reshape(4, 256, 16, 64)]
  transfers between devices with their start and end apart: 4 -> 0, of which waited for: 3 -> 0; matrix products, arithmetic and copies ran while one was open for 13% -> 0% of each run, Pallas kernels for 0% -> 0%
where the time goes in v1:
time: 219 us; the launch traced here: 218 us
  Pallas kernels  152 us (69%)
  matrix products  39.7 us (18%)
  local copies, waits for them, and re-layouts  23.2 us (11%)
  other arithmetic  3.77 us (2%)
    pallas_call x1, Pallas kernels, fetch(): pl.pallas_call(in_kernel, name='fetch', out_shape=(jax.ShapeDtypeStruct((...  117 us
    pallas_call x1, Pallas kernels, give(): pl.pallas_call(out_kernel, name='give', out_shape=jax.ShapeDtypeStruct((6...  19 us
    pallas_call x1, Pallas kernels, swap(): pl.pallas_call(swap_kernel, name='swap', out_shape=jax.ShapeDtypeStruct((...  15.3 us
    dot_general x1, matrix products, per_device(): jnp.einsum('chqk,ckhd->cqhd', w, v, preferred_element_type=F32).astype(BF)  13.5 us
    dot_general x1, matrix products, per_device(): part = jnp.einsum('ptkh,khd->ptd', hidden, down, preferred_element_type=F32)  10.5 us
    dot_general x1, matrix products, per_device(): jnp.einsum('td,sde->ste', near.reshape(1024, 1024), w_keyval, preferred_e...  7.32 us
    another operation x1, local copies, waits for them, and re-layouts, per_device(): v = kv[1].reshape(4, 256, 16, 64)  6.37 us
    unnamed x15, local copies, waits for them, and re-layouts  6.16 us

profile of v1, /device:TPU:1, one launch (start us, length us, event | category | flops | bytes accessed | tf_op | source)
XLA Modules:
  0.0 218.4 jit_solution(16838606004351793439)
XLA Ops:
  0.0 0.1 add_select_fusion
  0.1 0.8 copy.30
  0.9 0.1 reshape.100
  1.0 0.2 convert_reduce_fusion
  1.2 0.0 copy-start.4
  1.2 0.8 copy.31
  2.0 0.1 broadcast_in_dim.50
  2.1 0.4 select_reduce_fusion
  2.5 0.6 broadcast_in_dim.53.want
  3.1 0.0 copy-done.4
  3.1 117.2 %fetch.1 = (bf16[2,1024,256]{2,1,0:T(8,128)(2,1)}, bf16[8,1024,256]{2,1,0:T(8,128)(2,1)}, bf16[8,256,1024]{2,1,0:T(8,128)(2,1)}, bf16[16,64,1024]{2,1,0:T(8,128)...) custom-call(s32[128]{0:T(128)} %copy-done.4, s32[8,8,128]{2,1,0:T(8,128)} %broadcast_in_dim.53.want, ...), custom_call_target="tpu_custom_call" | custom-call | tf_op jit(solution)/shard_map/fetch/pallas_call | solution.py:186
  120.3 0.0 copy-start.1
  120.3 10.5 %fusion.73 = (bf16[2,256,1024]{2,1,0:T(8,128)(2,1)}, f32[2,256,1024]{2,1,0:T(8,128)}) fusion(bf16[8,256,1024]{2,1,0:T(8,128)(2,1)} %get-tuple-element.13, bf16[8,1024,256]{2,1,0:T(8,128)(2,1)} %get-tuple-element.12, bf16[2,1024,256]{2,1,0:T(8,128)(2,1)} %get-tuple-element.11), kind=kOutput, calls=%fused_computation.67 | convolution fusion | flops 4304928768 | bytes 12582912 | tf_op jit(solution)/shard_map/ptkh,khd->ptd/dot_general | solution.py:291
  130.8 0.0 copy-done.1
  130.8 0.0 copy-start.5
  130.8 0.7 copy.32
  131.5 15.3 %swap.1 = bf16[256,1024]{1,0:T(8,128)(2,1)} custom-call(bf16[2,256,1024]{2,1,0:T(8,128)(2,1)} %get-tuple-element.21.part), custom_call_target="tpu_custom_call" | custom-call | tf_op jit(solution)/shard_map/swap/pallas_call | solution.py:227
  146.8 1.7 fusion.40
  148.5 0.0 copy-start.2
  148.6 0.8 copy-done.2
  149.3 0.0 copy-done.5
  149.3 2.3 %convolution_convert_fusion = bf16[256,1024]{1,0:T(8,128)(2,1)S(1)} fusion(bf16[1024,1024]{1,0:T(8,128)(2,1)} %bitcast.74, bf16[256,1024]{1,0:T(8,128)(2,1)S(1)} %get-tuple-element.18, f32[1024]{0:T(1024)S(1)} %copy-done.5, f32[256]{0:T(256)S(1)} %add_rsqrt_fusion), kind=kOutput, calls=%fused_computation.36 | convolution fusion | flops 538181632 | bytes 3150848 | tf_op jit(solution)/shard_map/td,ed->te/dot_general | solution.py:299
  151.7 0.7 reshape.103
  152.3 7.3 %convert_bitcast_fusion = bf16[2,1024,1024]{2,1,0:T(8,128)(2,1)S(1)} fusion(bf16[1024,1024,1]{1,0,2:T(8,128)(2,1)} %bitcast.73, bf16[2,1024,1024]{2,1,0:T(8,128)(2,1)} %param.15), kind=kOutput, calls=%fused_computation.20 | convolution fusion | flops 4297064448 | bytes 10485760 | tf_op jit(solution)/shard_map/td,sde->ste/dot_general | solution.py:300
  159.7 1.8 fusion.72
  161.4 6.4 %reshape.113 = bf16[4,256,16,64]{3,2,1,0:T(8,128)(2,1)} reshape(bf16[1,1024,1024]{2,1,0:T(8,128)(2,1)} %get-tuple-element.19) | data formatting | bytes 4194304 | tf_op jit(solution)/shard_map/reshape;squeeze | solution.py:302
  167.8 4.0 %reshape.114 = bf16[4,256,16,64]{3,2,1,0:T(8,128)(2,1)} reshape(bf16[1,1024,1024]{2,1,0:T(8,128)(2,1)S(1)} %get-tuple-element.20) | data formatting | bytes 4194304 | tf_op jit(solution)/shard_map/reshape;squeeze | solution.py:301
  171.8 3.8 %fusion.9 = f32[4,16,64,256]{3,2,1,0:T(8,128)S(1)} fusion(bf16[4,256,16,64]{3,2,1,0:T(8,128)(2,1)} %reshape.114, bf16[4,64,16,64]{3,2,1,0:T(8,128)(2,1)S(1)} %reshape.103), kind=kOutput, calls=%fused_computation.10 | convolution fusion | flops 134217728 | bytes 6815744 | tf_op jit(solution)/shard_map/cqhd,ckhd->chqk/dot_general | solution.py:304
  175.6 0.0 copy-start
  175.6 2.0 copy-done
  177.5 1.4 fusion.78
  179.0 0.0 copy-start.3
  179.0 13.5 %fusion.35 = bf16[4,64,16,64]{1,3,2,0:T(8,128)(2,1)S(1)} fusion(f32[4,16,64]{2,1,0:T(8,128)S(1)} %fusion.78, bf16[4,256,16,64]{3,2,1,0:T(8,128)(2,1)} %reshape.113, f32[4,16,64,256]{3,2,1,0:T(8,128)} %copy-done), kind=kOutput, calls=%fused_computation.34 | convolution fusion | flops 139727104 | bytes 6832128 | tf_op jit(solution)/shard_map/chqk,ckhd->cqhd/dot_general | solution.py:306
  192.5 1.0 copy.39
  193.5 0.7 reshape.104
  194.2 0.0 copy-done.3
  194.2 2.3 %fusion.39 = bf16[1024,256]{0,1:T(8,128)(2,1)S(1)} fusion(bf16[256,1024]{1,0:T(8,128)(2,1)S(1)} %reshape.104, bf16[1024,1024]{1,0:T(8,128)(2,1)} %bitcast.72, bf16[256,1024]{1,0:T(8,128)(2,1)S(1)} %copy-done.3), kind=kOutput, calls=%fused_computation.37 | convolution fusion | flops 537657344 | bytes 3670016 | tf_op jit(solution)/shard_map/dot_general | solution.py:307
  196.5 1.0 copy.40
  197.5 19.0 %give.1 = bf16[64,4096]{1,0:T(8,128)(2,1)} custom-call(bf16[16,64,256]{2,1,0:T(8,128)(2,1)} %bitcast.68), custom_call_target="tpu_custom_call" | custom-call | tf_op jit(solution)/shard_map/give/pallas_call | solution.py:260
  216.6 1.9 copy.60
  (5 shorter events, 0.0 us)
Async XLA Ops:
  1.2 1.9 copy-start.4
  120.3 10.5 %copy-start.1 = (bf16[2,1024,256]{2,1,0:T(8,128)(2,1)S(1)}, bf16[2,1024,256]{2,1,0:T(8,128)(2,1)}, u32[]{:S(2)}) copy-start(bf16[2,1024,256]{2,1,0:T(8,128)(2,1)} %get-tuple-element.11) | copy-start | bytes 3145732
  130.8 18.5 %copy-start.5 = (f32[1024]{0:T(1024)S(1)}, f32[1024]{0:T(1024)}, u32[]{:S(2)}) copy-start(f32[1024]{0:T(1024)} %param.13) | copy-start | bytes 12292
  148.5 0.8 copy-start.2
  175.6 2.0 copy-start
  179.0 15.2 %copy-start.3 = (bf16[256,1024]{1,0:T(8,128)(2,1)S(1)}, bf16[256,1024]{1,0:T(8,128)(2,1)}, u32[]{:S(2)}) copy-start(bf16[256,1024]{1,0:T(8,128)(2,1)} %copy-done.2) | copy-start | bytes 1572868

commit v2 on v0

v2 whole, which is shorter than its diff:
```python
import jax
import jax.numpy as jnp
from jax import lax
from jax.experimental import pallas as pl
from jax.experimental.pallas import tpu as pltpu
from jax.sharding import PartitionSpec as P

MESH = pl.DeviceIdType.MESH
BF = jnp.bfloat16
F32 = jnp.float32
ANY = pl.BlockSpec(memory_space=pl.ANY)
VM = pl.BlockSpec(memory_space=pltpu.VMEM)
SM = pl.BlockSpec(memory_space=pltpu.SMEM)
CHUNKS = 4
WIDE = 1024 // CHUNKS


def remote(src, dst, send, recv, dev):
    return pltpu.make_async_remote_copy(
        src_ref=src, dst_ref=dst, send_sem=send, recv_sem=recv, device_id=dev, device_id_type=MESH
    )


def dot(a, b, dims):
    return lax.dot_general(a, b, (dims, ((), ())), preferred_element_type=F32)


def step_kernel(
    slot, want, gain, qt, up, down, wqt, wo, wkv, base,
    out,
    basev, sbuf, rbuf0, rbuf1, rbuf2, rbuf3, pbuf, near, xbuf, xtok, upall, downall, wqall, woall, wkvv,
    part, psend, precv, encoded, query, acc, ctx, outt, asked, asked_s,
    base_sem, ask_s, ask_r, ask_l, q_s, q_r, q_l, w_s, w_r, w_l, f_s, f_r, h_s, h_r, hf_s, hf_r,
    a_s, a_r, b_s, b_r, b_l, p_s, p_r, g_s, g_r, g_l,
):
    rbuf = (rbuf0, rbuf1, rbuf2, rbuf3)
    d = lax.axis_index("db")
    t = lax.axis_index("tp")
    xlo, y, xhi, c = d % 2, t // 4, (t // 2) % 2, t % 2
    sib = t + 1 - 2 * c
    flip = t + 2 - 4 * xhi
    load = pltpu.make_async_copy(base, basev, base_sem)
    load.start()
    near_peers = [lax.rem(d + k, 8) for k in (4, 2, 6)]
    lo_peers = [lax.rem(d + k, 8) + 1 - 2 * xlo for k in (4, 2, 6, 0)]
    db_peers = near_peers + lo_peers
    tp_peers = [lax.rem(t + k, 16) for k in range(1, 16)]
    y_peers = [lax.rem(t + 4 * k, 16) for k in (1, 3, 2)]
    across = (d + 1 - 2 * xlo, flip)

    sem = pltpu.get_barrier_semaphore()
    greeted = [(g, t) for g in db_peers] + [(d, s) for s in tp_peers] + [(g, flip) for g in lo_peers]
    for peer in greeted:
        pl.semaphore_signal(sem, inc=1, device_id=peer, device_id_type=MESH)
    pl.semaphore_wait(sem, len(greeted))

    waits = []
    asks = []
    for i, g in enumerate(db_peers):
        cp = remote(want.at[g], asked.at[d], ask_s.at[i], ask_r.at[d], (g, t))
        cp.start()
        asks.append((cp, g))
    own_ask = pltpu.make_async_copy(want.at[d], asked.at[d], ask_l.at[0])
    own_ask.start()

    mine = 2 * y + c
    weights = lambda ys, core: (
        (wqt, wqall, 4 * ys + 2 * xhi + core), (wo, woall, 4 * ys + 2 * xhi + core),
        (up, upall, 2 * ys + core), (down, downall, 2 * ys + core))
    for j, (src, dst, at) in enumerate(weights(y, c)):
        for i, s in enumerate(y_peers):
            cp = remote(src, dst.at[at], w_s.at[4 * i + j], w_r.at[4 * y + j], (d, s))
            cp.start()
            waits.append(cp.wait_send)
    own = []
    for j, (src, dst, at) in enumerate(weights(y, c)):
        cp = pltpu.make_async_copy(src, dst.at[at], w_l.at[j])
        cp.start()
        own.append(cp)
        cp = remote(src, dst.at[at], f_s.at[4 * y + j], f_r.at[4 * y + j], (d, sib))
        cp.start()
        waits.append(cp.wait_send)
        if j < 2:
            cp = remote(src, dst.at[at], h_s.at[2 * y + j], h_r.at[2 * y + j], across)
            cp.start()
            waits.append(cp.wait_send)

    feat = lambda s: pl.ds(pl.multiple_of(64 * s, 64), 64)
    for i, s in enumerate(tp_peers):
        to = (s // 4) * 4 + s % 2
        for p in range(2):
            col = pl.multiple_of(256 * (to + 2 * p), 256)
            cp = remote(
                qt.at[:, pl.ds(col, 256)], xbuf.at[p, feat(t), :],
                q_s.at[2 * i + p], q_r.at[2 * t + p], (d, s))
            cp.start()
            waits.append(cp.wait_send)
    for p in range(2):
        col = pl.multiple_of(256 * (4 * y + c + 2 * p), 256)
        cp = pltpu.make_async_copy(
            qt.at[:, pl.ds(col, 256)], xbuf.at[p, feat(t), :], q_l.at[p])
        cp.start()
        own.append(cp)
    cp = pltpu.make_async_copy(wkv, wkvv, w_l.at[4])
    cp.start()
    own.append(cp)

    own_ask.wait()
    for cp, g in asks:
        cp.wait_send()
        remote(want.at[d], asked.at[g], ask_s.at[0], ask_r.at[g], (g, t)).wait_recv()
    to_s = pltpu.make_async_copy(asked, asked_s, ask_l.at[1])
    to_s.start()
    to_s.wait()
    load.wait()

    def pack(f, g, dst):
        def body(r, carry):
            dst[f, g, r] = basev[asked_s[g, 0, r], :, WIDE * f:WIDE * (f + 1)].astype(BF)
            return carry
        lax.fori_loop(0, 32, body, 0, unroll=8)

    def pack_own(f):
        def body(r, carry):
            rbuf[f][d, r] = basev[asked_s[d, 0, r], :, WIDE * f:WIDE * (f + 1)].astype(BF)
            return carry
        lax.fori_loop(0, 32, body, 0, unroll=8)

    def first_pieces(f):
        pieces = [(pl.ds(0, 32), g, t, 0) for g in near_peers]
        for g in lo_peers:
            pieces += [(pl.ds(0, 16), g, t, 0), (pl.ds(16, 16), g, flip, 1)]
        return pieces

    for f in range(CHUNKS):
        n = 0
        for k, g in enumerate(db_peers):
            pack(f, g, sbuf)
            for rows, to, at, half in first_pieces(f):
                if to is g:
                    cp = remote(
                        sbuf.at[f, g, rows], rbuf[f].at[d, rows],
                        a_s.at[11 * f + n], a_r.at[16 * f + 2 * d + half], (g, at))
                    cp.start()
                    waits.append(cp.wait_send)
                    n += 1
        pack_own(f)

    for cp in own:
        cp.wait()
    for s in tp_peers:
        for p in range(2):
            remote(
                qt.at[:, pl.ds(0, 256)], xbuf.at[p, feat(s), :],
                q_s.at[0], q_r.at[2 * s + p], (d, s)).wait_recv()
    for p in range(2):
        xtok[p] = xbuf[p].astype(F32).T.astype(BF)

    def feed(at, first):
        def body(p, carry):
            h = dot(xtok[p], upall[at], ((1,), (0,)))
            h = jax.nn.gelu(h, approximate=True).astype(BF)
            term = dot(h, downall[at], ((1,), (0,)))
            if first:
                part[p] = term
            else:
                part[p] += term
            return carry
        lax.fori_loop(0, 2, body, 0)

    def from_sibling(ys, js):
        for j, (src, dst, at) in enumerate(weights(ys, 1 - c)):
            if j in js:
                remote(src, dst.at[at], f_s.at[0], f_r.at[4 * ys + j], (d, sib)).wait_recv()

    def from_y(s, js):
        ys = s // 4
        for j, (src, dst, at) in enumerate(weights(ys, c)):
            if j not in js:
                continue
            remote(src, dst.at[at], w_s.at[0], w_r.at[4 * ys + j], (d, s)).wait_recv()
            cp = remote(dst.at[at], dst.at[at], f_s.at[4 * ys + j], f_r.at[4 * ys + j], (d, sib))
            cp.start()
            waits.append(cp.wait_send)
            if j < 2:
                cp = remote(dst.at[at], dst.at[at], h_s.at[2 * ys + j], h_r.at[2 * ys + j], across)
                cp.start()
                waits.append(cp.wait_send)

    def second(f):
        for rows, g, at, half in first_pieces(f):
            remote(
                sbuf.at[f, g, rows], rbuf[f].at[g, rows],
                a_s.at[0], a_r.at[16 * f + 2 * g + half], (g, at)).wait_recv()
        for i, s in enumerate(tp_peers + [t]):
            for b in range(8):
                k = slot[s * 8 + b]
                pbuf[f, s, b // 2, 8 * (b % 2):8 * (b % 2) + 8, :] = rbuf[f][k // 32, k % 32]
            if i < 15:
                cp = remote(pbuf.at[f, s], near.at[f, :, t], b_s.at[15 * f + i], b_r.at[16 * f + t], (d, s))
                cp.start()
                waits.append(cp.wait_send)
        cp = pltpu.make_async_copy(pbuf.at[f, t], near.at[f, :, t], b_l.at[f])
        cp.start()
        local.append(cp)

    local = []
    for s in y_peers:
        from_y(s, (0, 1))
    feed(mine, True)
    from_sibling(y, (2, 3))
    feed(2 * y + 1 - c, False)
    second(0)
    from_y(y_peers[0], (2, 3))
    from_y(y_peers[1], (2, 3))
    feed(2 * (y_peers[0] // 4) + c, False)
    feed(2 * (y_peers[1] // 4) + c, False)
    for i in range(2):
        ys = y_peers[i] // 4
        from_sibling(ys, (2, 3))
        feed(2 * ys + 1 - c, False)
    second(1)
    from_y(y_peers[2], (2, 3))
    ys = y_peers[2] // 4
    feed(2 * ys + c, False)
    from_sibling(ys, (2, 3))
    feed(2 * ys + 1 - c, False)
    psend[...] = part[1 - xhi].astype(BF)
    swap = remote(psend, precv, p_s, p_r, (d, flip))
    swap.start()
    second(2)
    for ys in range(4):
        for j, (src, dst) in enumerate(((wqt, wqall), (wo, woall))):
            at = 4 * ys + 2 * (1 - xhi) + c
            remote(src, dst.at[at], h_s.at[0], h_r.at[2 * ys + j], across).wait_recv()
            cp = remote(dst.at[at], dst.at[at], hf_s.at[2 * ys + j], hf_r.at[2 * ys + j], (d, sib))
            cp.start()
            waits.append(cp.wait_send)
    second(3)

    swap.wait()
    enc = (xtok[xhi].astype(F32) + (part[xhi] + precv[...].astype(F32))).astype(BF).astype(F32)
    encoded[...] = enc
    scale = lax.rsqrt(jnp.mean(enc * enc, axis=1, keepdims=True) + 1e-06)
    normed = (enc * scale * gain[...]).astype(BF)
    for ys in range(4):
        from_sibling(ys, (0, 1))
        for j, (src, dst) in enumerate(((wqt, wqall), (wo, woall))):
            at = 4 * ys + 2 * (1 - xhi) + 1 - c
            remote(src, dst.at[at], hf_s.at[0], hf_r.at[2 * ys + j], (d, sib)).wait_recv()
    for e in range(4):
        wpart = wqall[4 * e:4 * e + 4].reshape(256, 1024)
        query[:, 256 * e:256 * e + 256] = (dot(normed, wpart, ((1,), (1,))) * 0.125).astype(BF)

    for f in range(CHUNKS):
        for s in tp_peers:
            remote(pbuf.at[f, s], near.at[f, :, s], b_s.at[0], b_r.at[16 * f + s], (d, s)).wait_recv()
        local[f].wait()
        for n in range(8):
            cols = slice(256 * (n % 4), 256 * (n % 4) + 256)
            full = slice(256 * n, 256 * n + 256)
            wpart = wkvv[n // 4, WIDE * f:WIDE * (f + 1), cols]

            def body(m, carry):
                rows = pl.ds(pl.multiple_of(256 * m, 256), 256)
                term = dot(near[f, m].reshape(256, WIDE), wpart, ((1,), (0,)))
                if f == 0:
                    acc[rows, full] = term
                else:
                    acc[rows, full] += term
                return carry
            lax.fori_loop(0, 4, body, 0)

    lane = lax.broadcasted_iota(jnp.int32, (1, 128), 1)
    low = (lane < 64).astype(F32).astype(BF)
    high = (lane >= 64).astype(F32).astype(BF)
    give = []
    for half in range(2):
        def body(m, carry):
            qrows = pl.ds(pl.multiple_of(64 * m, 64), 64)
            krows = pl.ds(pl.multiple_of(256 * m, 256), 256)
            for pair in range(8):
                cols = slice(128 * pair, 128 * pair + 128)
                vcols = slice(1024 + 128 * pair, 1024 + 128 * pair + 128)
                qp = query[qrows, cols]
                both = jnp.concatenate([qp * low, qp * high], axis=0)
                s = dot(both, acc[krows, cols].astype(BF), ((1,), (1,)))
                e = jnp.exp(s - jnp.max(s, axis=1, keepdims=True))
                total = jnp.sum(e, axis=1, keepdims=True)
                o = dot(e.astype(BF), acc[krows, vcols].astype(BF), ((1,), (0,))) / total
                ctx[qrows, cols] = jnp.where(lane < 64, o[:64], o[64:]).astype(BF)
            return carry
        lax.fori_loop(2 * half, 2 * half + 2, body, 0)
        rows = slice(128 * half, 128 * half + 128)
        for e in range(4):
            cols = slice(256 * e, 256 * e + 256)
            wpart = woall[:, :, cols].reshape(1024, 256)
            m = encoded[rows, cols] + dot(ctx[rows, :], wpart, ((1,), (0,)))
            outt[half, cols, :] = m.T.astype(BF)
        at = pl.ds(pl.multiple_of(256 * t + 128 * half, 128), 128)
        for i, s in enumerate(tp_peers):
            cp = remote(
                outt.at[half, feat(s), :], out.at[:, at],
                g_s.at[15 * half + i], g_r.at[16 * half + t], (d, s))
            cp.start()
            waits.append(cp.wait_send)
        cp = pltpu.make_async_copy(outt.at[half, feat(t), :], out.at[:, at], g_l.at[half])
        cp.start()
        waits.append(cp.wait)
    for half in range(2):
        for s in tp_peers:
            at = pl.ds(pl.multiple_of(256 * s + 128 * half, 128), 128)
            remote(
                outt.at[half, feat(s), :], out.at[:, at],
                g_s.at[0], g_r.at[16 * half + s], (d, s)).wait_recv()
    for w in waits:
        w()


def step(slot, want, gain, qt, up, down, wqt, wo, wkv, base):
    D = pltpu.SemaphoreType.DMA
    V = pltpu.VMEM
    return pl.pallas_call(
        step_kernel,
        name="step",
        out_shape=jax.ShapeDtypeStruct((64, 4096), BF),
        in_specs=[SM, VM, VM, ANY, ANY, ANY, ANY, ANY, ANY, ANY],
        out_specs=ANY,
        scratch_shapes=[
            V((256, 8, 1024), F32),
            V((CHUNKS, 8, 32, 8, WIDE), BF),
            *(V((8, 32, 8, WIDE), BF) for _ in range(CHUNKS)),
            V((CHUNKS, 16, 4, 16, WIDE), BF),
            V((CHUNKS, 4, 16, 16, WIDE), BF),
            V((2, 1024, 256), BF),
            V((2, 256, 1024), BF),
            V((8, 1024, 256), BF),
            V((8, 256, 1024), BF),
            V((16, 64, 1024), BF),
            V((16, 64, 1024), BF),
            V((2, 1024, 1024), BF),
            V((2, 256, 1024), F32),
            V((256, 1024), BF),
            V((256, 1024), BF),
            V((256, 1024), F32),
            V((256, 1024), BF),
            V((1024, 2048), F32),
            V((256, 1024), BF),
            V((2, 1024, 128), BF),
            V((8, 8, 128), jnp.int32),
            pltpu.SMEM((8, 8, 128), jnp.int32),
            D, D((7,)), D((8,)), D((2,)), D((30,)), D((32,)), D((2,)),
            D((12,)), D((16,)), D((5,)), D((16,)), D((16,)),
            D((8,)), D((8,)), D((8,)), D((8,)),
            D((11 * CHUNKS,)), D((16 * CHUNKS,)), D((15 * CHUNKS,)), D((16 * CHUNKS,)), D((CHUNKS,)),
            D, D, D((30,)), D((32,)), D((2,)),
        ],
        compiler_params=pltpu.CompilerParams(
            collective_id=0, has_side_effects=True, vmem_limit_bytes=59 << 20
        ),
    )(slot, want, gain, qt, up, down, wqt, wo, wkv, base)


def per_device(
    queries, enc_up, enc_down, attn_gain, w_query, w_keyval, w_out, database, nb_owner, nb_row
):
    owners = nb_owner.reshape(128)
    rows = nb_row.reshape(128)
    i = jnp.arange(128)
    rank = jnp.sum(
        ((owners[:, None] == owners[None, :]) & (i[None, :] < i[:, None])).astype(jnp.int32), axis=1)
    slot = owners * 32 + rank
    lane = jnp.arange(128)
    key = jnp.where((lane < 32)[None, :], lane[None, :] + 32 * jnp.arange(8)[:, None], -1)
    want = jnp.sum(
        jnp.where(key[:, :, None] == slot[None, None, :], rows[None, None, :], 0), axis=2)
    want = jnp.broadcast_to(want[:, None, :], (8, 8, 128))
    out = step(
        slot, want, attn_gain[None, :], queries.T, enc_up, enc_down, w_query.T, w_out,
        w_keyval, database)
    return out.T


def solution(mesh):
    placed = (
        P("db", "tp"),
        P(None, "tp"),
        P("tp", None),
        P(),
        P(None, "tp"),
        P(),
        P("tp", None),
        P("db", "tp", None),
        P("db", None),
        P("db", None),
    )
    return jax.shard_map(
        per_device, mesh=mesh, in_specs=placed, out_specs=P("db", "tp"), check_vma=False
    )
```

time: 513 us -> 174 us (0.34)
  waiting for transfers between devices: 269 us -> 0 us
  Pallas kernels: 0 us -> 169 us
  blocking collectives: 112 us -> 0 us
  local copies, waits for them, and re-layouts: 53.6 us -> 4.3 us
  matrix products: 46.4 us -> 0 us
  between operations: 13.3 us -> 0.05 us
  other arithmetic: 12.3 us -> 0.64 us
    pallas_call x0 -> x1, Pallas kernels: none -> 169 us  [step(): pl.pallas_call(step_kernel, name='step', out_shape=jax.ShapeDtypeStruct((...]
    all_to_all x2 -> x0, blocking collectives: 112 us -> none  [the longest x1 100 us: per_device(): lax.all_to_all(keyval, 'tp', split_axis=3, concat_axis=2, tiled=True)]
    unnamed x4 -> x0, waiting for transfers between devices: 102 us -> none
    psum x1 -> x0, waiting for transfers between devices: 97.2 us -> none  [per_device(): lax.psum(partial_value.astype(jnp.bfloat16), 'tp').astype(jnp.float32)]
    all_gather x1 -> x0, waiting for transfers between devices: 70.3 us -> none  [per_device(): full_q = lax.all_gather(queries, 'tp', axis=1, tiled=True)]
    dot_general x6 -> x0, matrix products: 46.4 us -> none  [the longest x1 13.5 us: per_device(): jnp.einsum('chqk,ckhd->cqhd', weights, values, preferred_element_type=jnp...]
    slice x3 -> x0, local copies, waits for them, and re-layouts: 16.3 us -> none  [the longest x2 9.82 us: per_device(): keys = keyval[0].reshape(stretches, span, local_heads, HEAD_DIM)]
    convert_element_type x2 -> x0, local copies, waits for them, and re-layouts: 12 us -> none  [the longest x1 11.3 us: per_device(): keyval = jnp.einsum('mtd,sde->smte', neighbours, w_keyval, preferred_elem...]
  transfers between devices with their start and end apart: 4 -> 0, of which waited for: 3 -> 0; matrix products, arithmetic and copies ran while one was open for 13% -> 0% of each run, Pallas kernels for 0% -> 0%
where the time goes in v2:
time: 174 us
  Pallas kernels  169 us (97%)
  local copies, waits for them, and re-layouts  4.3 us (2%)
    pallas_call x1, Pallas kernels, step(): pl.pallas_call(step_kernel, name='step', out_shape=jax.ShapeDtypeStruct((...  169 us

profile of v2, /device:TPU:1, one launch (start us, length us, event | category | flops | bytes accessed | tf_op | source)
XLA Modules:
  0.0 173.9 jit_solution(14811484479413529478)
XLA Ops:
  0.0 0.1 add_select_fusion
  0.1 0.8 copy.15
  0.9 0.1 reshape.57
  1.0 0.2 convert_reduce_fusion
  1.2 0.0 copy-start
  1.2 0.8 copy.16
  2.0 0.1 broadcast_in_dim.44
  2.1 0.4 select_reduce_fusion
  2.5 0.6 broadcast_in_dim.47.want
  3.1 0.0 copy-done
  3.1 168.9 %step.1 = bf16[64,4096]{1,0:T(8,128)(2,1)} custom-call(s32[128]{0:T(128)} %copy-done, s32[8,8,128]{2,1,0:T(8,128)} %broadcast_in_dim.47.want, f32[1,1024]{1,0:T(1,128)} %bitcast.7, bf16[64,4096]{1,0:T(8,128)(2,1)} %bitcast.5, bf16[1024,256]{1,0:T(8,128)(2,1)} %up.1, bf16[256,1024]{1,0:T(8,128)(2,1)} %down.1, bf16[64,1024]{1,0:T(8,128)(2,1)} %bitcast.6, ...), custom_call_target="tpu_custom_call" | custom-call | tf_op jit(solution)/shard_map/step/pallas_call | solution.py:323
  172.0 1.9 %copy.18 = bf16[4096,64]{0,1:T(8,128)(2,1)} copy(bf16[4096,64]{0,1:T(8,128)(2,1)} %bitcast.4) | data formatting | bytes 1048576
  (3 shorter events, 0.0 us)
Async XLA Ops:
  1.2 1.9 %copy-start = (s32[128]{0:T(128)}, s32[128]{0:T(128)S(1)}, u32[]{:S(2)}) copy-start(s32[128]{0:T(128)S(1)} %multiply_add_fusion.slot) | copy-start | bytes 1540

commit v3 on v2

--- a/solution.py
+++ b/solution.py
@@ -30,7 +30,7 @@
     out,
     basev, sbuf, rbuf0, rbuf1, rbuf2, rbuf3, pbuf, near, xbuf, xtok, upall, downall, wqall, woall, wkvv,
     part, psend, precv, encoded, query, acc, ctx, outt, asked, asked_s,
-    base_sem, ask_s, ask_r, ask_l, q_s, q_r, q_l, w_s, w_r, w_l, f_s, f_r, h_s, h_r, hf_s, hf_r,
+    base_sem, ask_s, ask_r, ask_l, q_s, q_r, q_l, r_s, r_r, w_s, w_r, w_l, f_s, f_r, h_s, h_r, z_s, z_r, hf_s, hf_r,
     a_s, a_r, b_s, b_r, b_l, p_s, p_r, g_s, g_r, g_l,
 ):
     rbuf = (rbuf0, rbuf1, rbuf2, rbuf3)
@@ -63,12 +63,31 @@
     own_ask = pltpu.make_async_copy(want.at[d], asked.at[d], ask_l.at[0])
     own_ask.start()
 
+    feat = lambda s: pl.ds(pl.multiple_of(64 * s, 64), 64)
+    q_peers = [
+        4 * lax.rem(y + k // 2, 4) + 2 * xhi + lax.rem(c + k % 2, 2) for k in range(1, 8)]
+    q_at = lambda s: 4 * (s // 4) + 2 * (s % 2)
+    for i, s in enumerate(q_peers):
+        for p in range(2):
+            col = pl.multiple_of(256 * ((s // 4) * 4 + s % 2 + 2 * p), 256)
+            cp = remote(
+                qt.at[:, pl.ds(col, 256)], xbuf.at[p, feat(t), :],
+                q_s.at[2 * i + p], q_r.at[q_at(t) + p], (d, s))
+            cp.start()
+            waits.append(cp.wait_send)
+    own_q = []
+    for p in range(2):
+        col = pl.multiple_of(256 * (4 * y + c + 2 * p), 256)
+        cp = pltpu.make_async_copy(
+            qt.at[:, pl.ds(col, 256)], xbuf.at[p, feat(t), :], q_l.at[p])
+        cp.start()
+        own_q.append(cp)
     mine = 2 * y + c
     weights = lambda ys, core: (
         (wqt, wqall, 4 * ys + 2 * xhi + core), (wo, woall, 4 * ys + 2 * xhi + core),
         (up, upall, 2 * ys + core), (down, downall, 2 * ys + core))
     for j, (src, dst, at) in enumerate(weights(y, c)):
-        for i, s in enumerate(y_peers):
+        for i, s in enumerate(y_peers[:2]):
             cp = remote(src, dst.at[at], w_s.at[4 * i + j], w_r.at[4 * y + j], (d, s))
             cp.start()
             waits.append(cp.wait_send)
@@ -80,27 +99,6 @@
         cp = remote(src, dst.at[at], f_s.at[4 * y + j], f_r.at[4 * y + j], (d, sib))
         cp.start()
         waits.append(cp.wait_send)
-        if j < 2:
-            cp = remote(src, dst.at[at], h_s.at[2 * y + j], h_r.at[2 * y + j], across)
-            cp.start()
-            waits.append(cp.wait_send)
-
-    feat = lambda s: pl.ds(pl.multiple_of(64 * s, 64), 64)
-    for i, s in enumerate(tp_peers):
-        to = (s // 4) * 4 + s % 2
-        for p in range(2):
-            col = pl.multiple_of(256 * (to + 2 * p), 256)
-            cp = remote(
-                qt.at[:, pl.ds(col, 256)], xbuf.at[p, feat(t), :],
-                q_s.at[2 * i + p], q_r.at[2 * t + p], (d, s))
-            cp.start()
-            waits.append(cp.wait_send)
-    for p in range(2):
-        col = pl.multiple_of(256 * (4 * y + c + 2 * p), 256)
-        cp = pltpu.make_async_copy(
-            qt.at[:, pl.ds(col, 256)], xbuf.at[p, feat(t), :], q_l.at[p])
-        cp.start()
-        own.append(cp)
     cp = pltpu.make_async_copy(wkv, wkvv, w_l.at[4])
     cp.start()
     own.append(cp)
@@ -132,29 +130,13 @@
             pieces += [(pl.ds(0, 16), g, t, 0), (pl.ds(16, 16), g, flip, 1)]
         return pieces
 
-    for f in range(CHUNKS):
-        n = 0
-        for k, g in enumerate(db_peers):
-            pack(f, g, sbuf)
-            for rows, to, at, half in first_pieces(f):
-                if to is g:
-                    cp = remote(
-                        sbuf.at[f, g, rows], rbuf[f].at[d, rows],
-                        a_s.at[11 * f + n], a_r.at[16 * f + 2 * d + half], (g, at))
-                    cp.start()
-                    waits.append(cp.wait_send)
-                    n += 1
-        pack_own(f)
-
-    for cp in own:
-        cp.wait()
-    for s in tp_peers:
+    def tokens():
+        for k in range(4):
+            for p in range(2):
+                block = xbuf.at[p, pl.ds(pl.multiple_of(256 * k + 128 * (1 - xhi), 128), 128), :]
+                remote(block, block, r_s.at[0], r_r.at[2 * k + p], (d, flip)).wait_recv()
         for p in range(2):
-            remote(
-                qt.at[:, pl.ds(0, 256)], xbuf.at[p, feat(s), :],
-                q_s.at[0], q_r.at[2 * s + p], (d, s)).wait_recv()
-    for p in range(2):
-        xtok[p] = xbuf[p].astype(F32).T.astype(BF)
+            xtok[p] = xbuf[p].astype(F32).T.astype(BF)
 
     def feed(at, first):
         def body(p, carry):
@@ -173,19 +155,67 @@
             if j in js:
                 remote(src, dst.at[at], f_s.at[0], f_r.at[4 * ys + j], (d, sib)).wait_recv()
 
-    def from_y(s, js):
-        ys = s // 4
+    def from_y(i, js):
+        ys = y_peers[i] // 4
         for j, (src, dst, at) in enumerate(weights(ys, c)):
             if j not in js:
                 continue
-            remote(src, dst.at[at], w_s.at[0], w_r.at[4 * ys + j], (d, s)).wait_recv()
+            remote(src, dst.at[at], w_s.at[0], w_r.at[4 * ys + j], (d, y_peers[i])).wait_recv()
+            if i < 2 and j % 2 == i:
+                cp = remote(
+                    dst.at[at], dst.at[at], w_s.at[8 + j], w_r.at[4 * ys + j], (d, y_peers[1 - i]))
+                cp.start()
+                waits.append(cp.wait_send)
             cp = remote(dst.at[at], dst.at[at], f_s.at[4 * ys + j], f_r.at[4 * ys + j], (d, sib))
             cp.start()
             waits.append(cp.wait_send)
-            if j < 2:
-                cp = remote(dst.at[at], dst.at[at], h_s.at[2 * ys + j], h_r.at[2 * ys + j], across)
+
+    def pass_tokens():
+        for cp in own_q:
+            cp.wait()
+        for s in q_peers:
+            for p in range(2):
+                remote(
+                    qt.at[:, pl.ds(0, 256)], xbuf.at[p, feat(s), :],
+                    q_s.at[0], q_r.at[q_at(s) + p], (d, s)).wait_recv()
+        for k in range(4):
+            for p in range(2):
+                block = xbuf.at[p, pl.ds(pl.multiple_of(256 * k + 128 * xhi, 128), 128), :]
+                cp = remote(block, block, r_s.at[2 * k + p], r_r.at[2 * k + p], (d, flip))
                 cp.start()
                 waits.append(cp.wait_send)
+
+    z = d // 2
+    cross = (wqall, woall)
+
+    def across_send():
+        for j, dst in enumerate(cross):
+            at = 4 * z + 2 * xhi + c
+            cp = remote(dst.at[at], dst.at[at], h_s.at[j], h_r.at[j], across)
+            cp.start()
+            waits.append(cp.wait_send)
+
+    def to_sibling(zz, j, piece):
+        cp = remote(piece, piece, hf_s.at[2 * zz + j], hf_r.at[2 * zz + j], (d, sib))
+        cp.start()
+        waits.append(cp.wait_send)
+
+    def across_recv():
+        for j, dst in enumerate(cross):
+            piece = dst.at[4 * z + 2 * (1 - xhi) + c]
+            remote(piece, piece, h_s.at[0], h_r.at[j], across).wait_recv()
+            for i, g in enumerate(near_peers):
+                cp = remote(piece, piece, z_s.at[2 * i + j], z_r.at[2 * z + j], (g, t))
+                cp.start()
+                waits.append(cp.wait_send)
+            to_sibling(z, j, piece)
+
+    def from_z():
+        for g in near_peers:
+            for j, dst in enumerate(cross):
+                piece = dst.at[4 * (g // 2) + 2 * (1 - xhi) + c]
+                remote(piece, piece, z_s.at[0], z_r.at[2 * (g // 2) + j], (g, t)).wait_recv()
+                to_sibling(g // 2, j, piece)
 
     def second(f):
         for rows, g, at, half in first_pieces(f):
@@ -204,73 +234,90 @@
         cp.start()
         local.append(cp)
 
+    def keyval(f):
+        for s in tp_peers:
+            remote(pbuf.at[f, s], near.at[f, :, s], b_s.at[0], b_r.at[16 * f + s], (d, s)).wait_recv()
+        local[f].wait()
+
+        def body(n, carry):
+            cols = pl.ds(pl.multiple_of(256 * lax.rem(n, 4), 256), 256)
+            full = pl.ds(pl.multiple_of(256 * n, 256), 256)
+            wpart = wkvv[n // 4, WIDE * f:WIDE * (f + 1), cols]
+            term = dot(near[f].reshape(1024, WIDE), wpart, ((1,), (0,)))
+            if f == 0:
+                acc[:, full] = term
+            else:
+                acc[:, full] += term
+            return carry
+        lax.fori_loop(0, 8, body, 0)
+
+    for f in range(CHUNKS):
+        n = 0
+        for k, g in enumerate(db_peers):
+            pack(f, g, sbuf)
+            for rows, to, at, half in first_pieces(f):
+                if to is g:
+                    cp = remote(
+                        sbuf.at[f, g, rows], rbuf[f].at[d, rows],
+                        a_s.at[11 * f + n], a_r.at[16 * f + 2 * d + half], (g, at))
+                    cp.start()
+                    waits.append(cp.wait_send)
+                    n += 1
+        pack_own(f)
+        if f == 0:
+            pass_tokens()
+
     local = []
-    for s in y_peers:
-        from_y(s, (0, 1))
+    ys = [s // 4 for s in y_peers]
+    for cp in own:
+        cp.wait()
+    from_y(0, (0, 1))
+    from_y(1, (0, 1))
+    second(0)
+    from_y(2, (0, 1))
+    across_send()
+    tokens()
     feed(mine, True)
     from_sibling(y, (2, 3))
     feed(2 * y + 1 - c, False)
-    second(0)
-    from_y(y_peers[0], (2, 3))
-    from_y(y_peers[1], (2, 3))
-    feed(2 * (y_peers[0] // 4) + c, False)
-    feed(2 * (y_peers[1] // 4) + c, False)
+    second(1)
+    from_y(0, (2, 3))
+    from_y(1, (2, 3))
+    across_recv()
+    feed(2 * ys[0] + c, False)
+    feed(2 * ys[1] + c, False)
+    second(2)
+    keyval(0)
     for i in range(2):
-        ys = y_peers[i] // 4
-        from_sibling(ys, (2, 3))
-        feed(2 * ys + 1 - c, False)
-    second(1)
-    from_y(y_peers[2], (2, 3))
-    ys = y_peers[2] // 4
-    feed(2 * ys + c, False)
-    from_sibling(ys, (2, 3))
-    feed(2 * ys + 1 - c, False)
+        from_sibling(ys[i], (2, 3))
+        feed(2 * ys[i] + 1 - c, False)
+    from_z()
+    from_y(2, (2, 3))
+    second(3)
+    feed(2 * ys[2] + c, False)
+    from_sibling(ys[2], (2, 3))
+    feed(2 * ys[2] + 1 - c, False)
     psend[...] = part[1 - xhi].astype(BF)
     swap = remote(psend, precv, p_s, p_r, (d, flip))
     swap.start()
-    second(2)
-    for ys in range(4):
-        for j, (src, dst) in enumerate(((wqt, wqall), (wo, woall))):
-            at = 4 * ys + 2 * (1 - xhi) + c
-            remote(src, dst.at[at], h_s.at[0], h_r.at[2 * ys + j], across).wait_recv()
-            cp = remote(dst.at[at], dst.at[at], hf_s.at[2 * ys + j], hf_r.at[2 * ys + j], (d, sib))
-            cp.start()
-            waits.append(cp.wait_send)
-    second(3)
+    keyval(1)
+    keyval(2)
 
     swap.wait()
     enc = (xtok[xhi].astype(F32) + (part[xhi] + precv[...].astype(F32))).astype(BF).astype(F32)
     encoded[...] = enc
     scale = lax.rsqrt(jnp.mean(enc * enc, axis=1, keepdims=True) + 1e-06)
     normed = (enc * scale * gain[...]).astype(BF)
-    for ys in range(4):
-        from_sibling(ys, (0, 1))
+    for k in range(4):
+        from_sibling(k, (0, 1))
         for j, (src, dst) in enumerate(((wqt, wqall), (wo, woall))):
-            at = 4 * ys + 2 * (1 - xhi) + 1 - c
-            remote(src, dst.at[at], hf_s.at[0], hf_r.at[2 * ys + j], (d, sib)).wait_recv()
+            at = 4 * k + 2 * (1 - xhi) + 1 - c
+            remote(src, dst.at[at], hf_s.at[0], hf_r.at[2 * k + j], (d, sib)).wait_recv()
     for e in range(4):
         wpart = wqall[4 * e:4 * e + 4].reshape(256, 1024)
         query[:, 256 * e:256 * e + 256] = (dot(normed, wpart, ((1,), (1,))) * 0.125).astype(BF)
 
-    for f in range(CHUNKS):
-        for s in tp_peers:
-            remote(pbuf.at[f, s], near.at[f, :, s], b_s.at[0], b_r.at[16 * f + s], (d, s)).wait_recv()
-        local[f].wait()
-        for n in range(8):
-            cols = slice(256 * (n % 4), 256 * (n % 4) + 256)
-            full = slice(256 * n, 256 * n + 256)
-            wpart = wkvv[n // 4, WIDE * f:WIDE * (f + 1), cols]
-
-            def body(m, carry):
-                rows = pl.ds(pl.multiple_of(256 * m, 256), 256)
-                term = dot(near[f, m].reshape(256, WIDE), wpart, ((1,), (0,)))
-                if f == 0:
-                    acc[rows, full] = term
-                else:
-                    acc[rows, full] += term
-                return carry
-            lax.fori_loop(0, 4, body, 0)
-
+    keyval(3)
     lane = lax.broadcasted_iota(jnp.int32, (1, 128), 1)
     low = (lane < 64).astype(F32).astype(BF)
     high = (lane >= 64).astype(F32).astype(BF)
@@ -349,9 +396,9 @@
             V((2, 1024, 128), BF),
             V((8, 8, 128), jnp.int32),
             pltpu.SMEM((8, 8, 128), jnp.int32),
-            D, D((7,)), D((8,)), D((2,)), D((30,)), D((32,)), D((2,)),
+            D, D((7,)), D((8,)), D((2,)), D((14,)), D((16,)), D((2,)), D((8,)), D((8,)),
             D((12,)), D((16,)), D((5,)), D((16,)), D((16,)),
-            D((8,)), D((8,)), D((8,)), D((8,)),
+            D((2,)), D((2,)), D((6,)), D((8,)), D((8,)), D((8,)),
             D((11 * CHUNKS,)), D((16 * CHUNKS,)), D((15 * CHUNKS,)), D((16 * CHUNKS,)), D((CHUNKS,)),
             D, D, D((30,)), D((32,)), D((2,)),
         ],

time: 174 us -> 121 us (0.70)
  Pallas kernels: 169 us -> 116 us
    pallas_call x1, Pallas kernels: 169 us -> 116 us  [step(): pl.pallas_call(step_kernel, name='step', out_shape=jax.ShapeDtypeStruct((...]
where the time goes in v3:
time: 121 us
  Pallas kernels  116 us (96%)
  local copies, waits for them, and re-layouts  4.3 us (4%)
    pallas_call x1, Pallas kernels, step(): pl.pallas_call(step_kernel, name='step', out_shape=jax.ShapeDtypeStruct((...  116 us
    unnamed x5, local copies, waits for them, and re-layouts  3.41 us

profile of v3, /device:TPU:1, one launch (start us, length us, event | category | flops | bytes accessed | tf_op | source)
XLA Modules:
  0.0 120.6 jit_solution(11684883059670083259)
XLA Ops:
  0.0 0.1 add_select_fusion
  0.1 0.8 copy.15
  0.9 0.1 reshape.57
  1.0 0.2 convert_reduce_fusion
  1.2 0.0 copy-start
  1.2 0.8 copy.16
  2.0 0.1 broadcast_in_dim.44
  2.1 0.4 select_reduce_fusion
  2.5 0.6 broadcast_in_dim.47.want
  3.1 0.0 copy-done
  3.1 115.6 %step.1 = bf16[64,4096]{1,0:T(8,128)(2,1)} custom-call(s32[128]{0:T(128)} %copy-done, s32[8,8,128]{2,1,0:T(8,128)} %broadcast_in_dim.47.want, f32[1,1024]{1,0:T(1,128)} %bitcast.7, bf16[64,4096]{1,0:T(8,128)(2,1)} %bitcast.5, bf16[1024,256]{1,0:T(8,128)(2,1)} %up.1, bf16[256,1024]{1,0:T(8,128)(2,1)} %down.1, bf16[64,1024]{1,0:T(8,128)(2,1)} %bitcast.6, ...), custom_call_target="tpu_custom_call" | custom-call | tf_op jit(solution)/shard_map/step/pallas_call | solution.py:370
  118.7 1.9 %copy.18 = bf16[4096,64]{0,1:T(8,128)(2,1)} copy(bf16[4096,64]{0,1:T(8,128)(2,1)} %bitcast.4) | data formatting | bytes 1048576
  (3 shorter events, 0.0 us)
Async XLA Ops:
  1.2 1.9 %copy-start = (s32[128]{0:T(128)}, s32[128]{0:T(128)S(1)}, u32[]{:S(2)}) copy-start(s32[128]{0:T(128)S(1)} %multiply_add_fusion.slot) | copy-start | bytes 1540

commit v4 on v3

--- a/solution.py
+++ b/solution.py
@@ -86,11 +86,11 @@
     weights = lambda ys, core: (
         (wqt, wqall, 4 * ys + 2 * xhi + core), (wo, woall, 4 * ys + 2 * xhi + core),
         (up, upall, 2 * ys + core), (down, downall, 2 * ys + core))
-    for j, (src, dst, at) in enumerate(weights(y, c)):
-        for i, s in enumerate(y_peers[:2]):
-            cp = remote(src, dst.at[at], w_s.at[4 * i + j], w_r.at[4 * y + j], (d, s))
-            cp.start()
-            waits.append(cp.wait_send)
+    for i, j in ((0, 1), (1, 0), (0, 0), (1, 1), (0, 3), (1, 2), (0, 2), (1, 3)):
+        src, dst, at = weights(y, c)[j]
+        cp = remote(src, dst.at[at], w_s.at[4 * i + j], w_r.at[4 * y + j], (d, y_peers[i]))
+        cp.start()
+        waits.append(cp.wait_send)
     own = []
     for j, (src, dst, at) in enumerate(weights(y, c)):
         cp = pltpu.make_async_copy(src, dst.at[at], w_l.at[j])
@@ -240,16 +240,16 @@
         local[f].wait()
 
         def body(n, carry):
-            cols = pl.ds(pl.multiple_of(256 * lax.rem(n, 4), 256), 256)
-            full = pl.ds(pl.multiple_of(256 * n, 256), 256)
-            wpart = wkvv[n // 4, WIDE * f:WIDE * (f + 1), cols]
+            cols = pl.ds(pl.multiple_of(512 * lax.rem(n, 2), 512), 512)
+            full = pl.ds(pl.multiple_of(512 * n, 512), 512)
+            wpart = wkvv[n // 2, WIDE * f:WIDE * (f + 1), cols]
             term = dot(near[f].reshape(1024, WIDE), wpart, ((1,), (0,)))
             if f == 0:
                 acc[:, full] = term
             else:
                 acc[:, full] += term
             return carry
-        lax.fori_loop(0, 8, body, 0)
+        lax.fori_loop(0, 4, body, 0)
 
     for f in range(CHUNKS):
         n = 0
@@ -276,18 +276,19 @@
     second(0)
     from_y(2, (0, 1))
     across_send()
+    from_y(0, (2,))
+    from_y(1, (3,))
     tokens()
     feed(mine, True)
     from_sibling(y, (2, 3))
     feed(2 * y + 1 - c, False)
     second(1)
-    from_y(0, (2, 3))
-    from_y(1, (2, 3))
+    from_y(0, (3,))
+    from_y(1, (2,))
     across_recv()
     feed(2 * ys[0] + c, False)
     feed(2 * ys[1] + c, False)
     second(2)
-    keyval(0)
     for i in range(2):
         from_sibling(ys[i], (2, 3))
         feed(2 * ys[i] + 1 - c, False)
@@ -300,6 +301,7 @@
     psend[...] = part[1 - xhi].astype(BF)
     swap = remote(psend, precv, p_s, p_r, (d, flip))
     swap.start()
+    keyval(0)
     keyval(1)
     keyval(2)
 

time: 121 us -> 120 us (level)
  no operation moved by 1% of the time
where the time goes in v4:
time: 120 us
  Pallas kernels  115 us (96%)
  local copies, waits for them, and re-layouts  4.3 us (4%)
    pallas_call x1, Pallas kernels, step(): pl.pallas_call(step_kernel, name='step', out_shape=jax.ShapeDtypeStruct((...  115 us
    unnamed x5, local copies, waits for them, and re-layouts  3.41 us

profile of v4, /device:TPU:1, one launch (start us, length us, event | category | flops | bytes accessed | tf_op | source)
XLA Modules:
  0.0 119.9 jit_solution(8909955548688797760)
XLA Ops:
  0.0 0.1 add_select_fusion
  0.1 0.8 copy.15
  0.9 0.1 reshape.57
  1.0 0.2 convert_reduce_fusion
  1.2 0.0 copy-start
  1.2 0.8 copy.16
  2.0 0.1 broadcast_in_dim.44
  2.1 0.4 select_reduce_fusion
  2.5 0.6 broadcast_in_dim.47.want
  3.1 0.0 copy-done
  3.1 114.9 %step.1 = bf16[64,4096]{1,0:T(8,128)(2,1)} custom-call(s32[128]{0:T(128)} %copy-done, s32[8,8,128]{2,1,0:T(8,128)} %broadcast_in_dim.47.want, f32[1,1024]{1,0:T(1,128)} %bitcast.7, bf16[64,4096]{1,0:T(8,128)(2,1)} %bitcast.5, bf16[1024,256]{1,0:T(8,128)(2,1)} %up.1, bf16[256,1024]{1,0:T(8,128)(2,1)} %down.1, bf16[64,1024]{1,0:T(8,128)(2,1)} %bitcast.6, ...), custom_call_target="tpu_custom_call" | custom-call | tf_op jit(solution)/shard_map/step/pallas_call | solution.py:372
  118.0 1.9 %copy.18 = bf16[4096,64]{0,1:T(8,128)(2,1)} copy(bf16[4096,64]{0,1:T(8,128)(2,1)} %bitcast.4) | data formatting | bytes 1048576
  (3 shorter events, 0.0 us)
Async XLA Ops:
  1.2 1.9 %copy-start = (s32[128]{0:T(128)}, s32[128]{0:T(128)S(1)}, u32[]{:S(2)}) copy-start(s32[128]{0:T(128)S(1)} %multiply_add_fusion.slot) | copy-start | bytes 1540

commit v5 on v4

--- a/solution.py
+++ b/solution.py
@@ -251,6 +251,7 @@
             return carry
         lax.fori_loop(0, 4, body, 0)
 
+    pass_tokens()
     for f in range(CHUNKS):
         n = 0
         for k, g in enumerate(db_peers):
@@ -264,8 +265,6 @@
                     waits.append(cp.wait_send)
                     n += 1
         pack_own(f)
-        if f == 0:
-            pass_tokens()
 
     local = []
     ys = [s // 4 for s in y_peers]

time: 120 us -> 128 us (1.067)
  Pallas kernels: 115 us -> 123 us
    pallas_call x1, Pallas kernels: 115 us -> 123 us  [step(): pl.pallas_call(step_kernel, name='step', out_shape=jax.ShapeDtypeStruct((...]
where the time goes in v5:
time: 128 us
  Pallas kernels  123 us (96%)
  local copies, waits for them, and re-layouts  4.3 us (3%)
    pallas_call x1, Pallas kernels, step(): pl.pallas_call(step_kernel, name='step', out_shape=jax.ShapeDtypeStruct((...  123 us
    unnamed x5, local copies, waits for them, and re-layouts  3.41 us

profile of v5, /device:TPU:1, one launch (start us, length us, event | category | flops | bytes accessed | tf_op | source)
XLA Modules:
  0.0 128.2 jit_solution(1462085109704776602)
XLA Ops:
  0.0 0.1 add_select_fusion
  0.1 0.8 copy.15
  0.9 0.1 reshape.57
  1.0 0.2 convert_reduce_fusion
  1.2 0.0 copy-start
  1.2 0.8 copy.16
  2.0 0.1 broadcast_in_dim.44
  2.1 0.4 select_reduce_fusion
  2.5 0.6 broadcast_in_dim.47.want
  3.1 0.0 copy-done
  3.1 123.2 %step.1 = bf16[64,4096]{1,0:T(8,128)(2,1)} custom-call(s32[128]{0:T(128)} %copy-done, s32[8,8,128]{2,1,0:T(8,128)} %broadcast_in_dim.47.want, f32[1,1024]{1,0:T(1,128)} %bitcast.7, bf16[64,4096]{1,0:T(8,128)(2,1)} %bitcast.5, bf16[1024,256]{1,0:T(8,128)(2,1)} %up.1, bf16[256,1024]{1,0:T(8,128)(2,1)} %down.1, bf16[64,1024]{1,0:T(8,128)(2,1)} %bitcast.6, ...), custom_call_target="tpu_custom_call" | custom-call | tf_op jit(solution)/shard_map/step/pallas_call | solution.py:371
  126.3 1.9 %copy.18 = bf16[4096,64]{0,1:T(8,128)(2,1)} copy(bf16[4096,64]{0,1:T(8,128)(2,1)} %bitcast.4) | data formatting | bytes 1048576
  (3 shorter events, 0.0 us)
Async XLA Ops:
  1.2 1.9 %copy-start = (s32[128]{0:T(128)}, s32[128]{0:T(128)S(1)}, u32[]{:S(2)}) copy-start(s32[128]{0:T(128)S(1)} %multiply_add_fusion.slot) | copy-start | bytes 1540
